TPU v7x, 32 devices: a whole 2x2x4 slice. The times are simulated.
32 devices in a mesh: dp: 32 (over z, y, x, core).
Axes of the slice: x: 2, y: 2, z: 4, core: 2. Of those that a mesh axis runs over, the one named last changes fastest.
Arguments:
- tokens: bfloat16 [8192, 960], P('dp'), may hold values from -6 to 6
- out_grad: bfloat16 [8192, 960], P('dp'), may hold values from -6 to 6
- segment_ids: int32 [32, 256], P('dp'), may hold values from 0 to 255, as said below
- positions: int32 [32, 256], P('dp'), may hold values from 0 to 255, as said below
- attn_weight: bfloat16 [960, 2560], P(None, 'dp'), as said below
- gate_weight: bfloat16 [960, 2560], P(None, 'dp'), may hold values from -0.1875 to 0.1875
- up_weight: bfloat16 [960, 2560], P(None, 'dp'), may hold values from -0.1875 to 0.1875
- down_weight: bfloat16 [2560, 960], P('dp'), may hold values from -0.15625 to 0.15625
- norm_gains: bfloat16 [1920], P('dp'), may hold values from 0.25 to 1.75
Outputs:
- block_out: bfloat16 [8192, 960], P('dp')
- tokens_grad: float32 [8192, 960], P('dp')
- attn_weight_grad: float32 [960, 2560], P(None, 'dp')
- gate_weight_grad: float32 [960, 2560], P(None, 'dp')
- up_weight_grad: float32 [960, 2560], P(None, 'dp')
- down_weight_grad: float32 [2560, 960], P('dp')
- norm_gains_grad: float32 [1920], P('dp')
Inputs may be any that keep to these rules, and one draw needn't show every extreme that they name: `segment_ids`: in every sequence the ids start at 0 and rise by one where a new document begins; some sequence has a new document at every token. `positions`: A token's offset from the first token of its document; some sequence is a single document. `attn_weight`: projection weights scaled by their fan-in.
All inputs are finite; a program needn't handle non-finite values.
Results may differ from a plain program's by a relative error of at most 0.01.
The roundings to bfloat16 on the way count: a program that leaves them out, or rounds other values in their place, can miss the bound.
Values may be sent and summed in bfloat16 or wider, within the bound.
A program may use at most 256 MiB of HBM per device.

v0:
```python
import jax
import jax.numpy as jnp
from jax import lax
from jax.sharding import PartitionSpec as P

HEADS = 15
KV_HEADS = 5
HEAD_DIM = 64
GROUP = 3
QD = 960
KD = 320


epsilon = 1e-05
rope_base = 10000.0
masked_score = -1e30


def product(form, left, right):
    return jnp.einsum(form, left, right, preferred_element_type=jnp.float32)


def contract(left, right, left_axis, right_axis):
    return lax.dot_general(
        left, right, (((left_axis,), (right_axis,)), ((), ())), preferred_element_type=jnp.float32
    )


def rotate_half(values):
    half_dim = values.shape[-1] // 2
    return jnp.concatenate([-values[..., half_dim:], values[..., :half_dim]], axis=-1)


def rope_tables(positions):
    half_dim = HEAD_DIM // 2
    inverse = rope_base ** (-2.0 * jnp.arange(half_dim).astype(jnp.float32) / HEAD_DIM)
    angles = positions.astype(jnp.float32)[:, None] * inverse[None, :]
    angles = jnp.concatenate([angles, angles], axis=-1)
    return (jnp.cos(angles)[:, None, :], jnp.sin(angles)[:, None, :])


def norm_rows(values, gain):
    inv_rms = lax.rsqrt(jnp.mean(values * values, axis=-1, keepdims=True) + epsilon)
    normed = values * inv_rms
    return (normed, inv_rms, (normed * gain.astype(jnp.float32)).astype(jnp.bfloat16))


def norm_back(grad_in, normed, inv_rms, gain):
    grad_normed = grad_in * gain.astype(jnp.float32)
    grad_gain = jnp.sum(grad_in * normed, axis=0)
    inner_mean = jnp.mean(grad_normed * normed, axis=-1, keepdims=True)
    return (inv_rms * (grad_normed - normed * inner_mean), grad_gain)


def allowed_pairs(segments):
    row_index = jnp.arange(segments.shape[0])
    same_doc = segments[:, None] == segments[None, :]
    return same_doc & (row_index[:, None] >= row_index[None, :])


def scores_of(queries, key_rows, allowed):
    scores = product("qhgd,shd->hgqs", queries, key_rows) * HEAD_DIM ** (-0.5)
    return jnp.where(allowed[None, None], scores, masked_score)


def attend(queries, key_rows, value_rows, allowed):
    scores = scores_of(queries, key_rows, allowed)
    row_max = jnp.max(scores, axis=-1, keepdims=True)
    weights = jnp.exp(scores - row_max)
    totals = jnp.sum(weights, axis=-1, keepdims=True)
    weights_low = (weights / totals).astype(jnp.bfloat16)
    mixed_heads = product("hgqs,shd->qhgd", weights_low, value_rows).astype(jnp.bfloat16)
    return (mixed_heads, row_max + jnp.log(totals))


def attend_back(queries, key_rows, value_rows, allowed, mixed_heads, log_totals, grad_heads):
    scores = scores_of(queries, key_rows, allowed)
    probs_back = jnp.exp(scores - log_totals)
    grad_values = product("hgqs,qhgd->shd", probs_back.astype(jnp.bfloat16), grad_heads)
    grad_probs = product("qhgd,shd->hgqs", grad_heads, value_rows)
    row_dot = jnp.sum(grad_heads.astype(jnp.float32) * mixed_heads.astype(jnp.float32), axis=-1)
    row_dot = jnp.transpose(row_dot, (1, 2, 0))[..., None]
    grad_scores = (probs_back * (grad_probs - row_dot) * HEAD_DIM ** (-0.5)).astype(jnp.bfloat16)
    grad_queries = product("hgqs,shd->qhgd", grad_scores, key_rows)
    grad_keys = product("hgqs,qhgd->shd", grad_scores, queries)
    return (grad_queries, grad_keys, grad_values)


def layer_forward(
    tokens, segments, positions, attn_weight, gate_weight, up_weight, down_weight, norm_gains
):
    seq_len = tokens.shape[0]
    model_width = tokens.shape[1]
    residual = tokens.astype(jnp.float32)
    normed_one, inv_one, input_one = norm_rows(residual, norm_gains[:model_width])
    projected = contract(input_one, attn_weight[:, : QD + 2 * KD], 1, 0)
    cosine, sine_tab = rope_tables(positions)
    query_part = projected[:, :QD].reshape(seq_len, HEADS, HEAD_DIM)
    key_part = projected[:, QD : QD + KD].reshape(seq_len, KV_HEADS, HEAD_DIM)
    queries = (query_part * cosine + rotate_half(query_part) * sine_tab).astype(jnp.bfloat16)
    queries = queries.reshape(seq_len, KV_HEADS, GROUP, HEAD_DIM)
    key_rows = (key_part * cosine + rotate_half(key_part) * sine_tab).astype(jnp.bfloat16)
    value_rows = projected[:, QD + KD :].reshape(seq_len, KV_HEADS, HEAD_DIM).astype(jnp.bfloat16)
    allowed = allowed_pairs(segments)
    mixed_heads, log_totals = attend(queries, key_rows, value_rows, allowed)
    mixed_flat = mixed_heads.reshape(seq_len, QD)
    middle = residual + contract(mixed_flat, attn_weight[:, QD + 2 * KD :], 1, 1)
    normed_two, inv_two, input_two = norm_rows(middle, norm_gains[model_width:])
    gate_act = contract(input_two, gate_weight, 1, 0)
    up_proj = contract(input_two, up_weight, 1, 0)
    hidden = (jax.nn.silu(gate_act) * up_proj).astype(jnp.bfloat16)
    output = middle + contract(hidden, down_weight, 1, 0)
    kept_state = {
        "normed_one": normed_one,
        "inv_one": inv_one,
        "input_one": input_one,
        "cosine": cosine,
        "sine_tab": sine_tab,
        "queries": queries,
        "key_rows": key_rows,
        "value_rows": value_rows,
        "allowed": allowed,
        "mixed_heads": mixed_heads,
        "log_totals": log_totals,
        "normed_two": normed_two,
        "inv_two": inv_two,
        "input_two": input_two,
        "gate_act": gate_act,
        "up_proj": up_proj,
        "hidden": hidden,
    }
    return (output.astype(jnp.bfloat16), kept_state)


def ffn_backward(out_grad, kept_state, gate_weight, up_weight, down_weight, norm_gains):
    model_width = out_grad.shape[1]
    gate_act = kept_state["gate_act"]
    input_two = kept_state["input_two"]
    grad_hidden = contract(out_grad, down_weight, 1, 1)
    grad_down = contract(kept_state["hidden"], out_grad, 0, 0)
    sig_gate = jax.nn.sigmoid(gate_act)
    grad_gate = (
        grad_hidden * kept_state["up_proj"] * sig_gate * (1.0 + gate_act * (1.0 - sig_gate))
    ).astype(jnp.bfloat16)
    grad_up = (grad_hidden * gate_act * sig_gate).astype(jnp.bfloat16)
    grad_gate_w = contract(input_two, grad_gate, 0, 0)
    grad_up_w = contract(input_two, grad_up, 0, 0)
    grad_input_two = contract(grad_gate, gate_weight, 1, 1) + contract(grad_up, up_weight, 1, 1)
    grad_norm_two, grad_gain_two = norm_back(
        grad_input_two, kept_state["normed_two"], kept_state["inv_two"], norm_gains[model_width:]
    )
    grad_middle = out_grad.astype(jnp.float32) + grad_norm_two
    return (grad_middle, grad_gain_two, (grad_gate_w, grad_up_w, grad_down))


def attn_backward(grad_middle, kept_state, attn_weight, norm_gains):
    seq_len = grad_middle.shape[0]
    model_width = grad_middle.shape[1]
    mixed_heads = kept_state["mixed_heads"]
    grad_mid_low = grad_middle.astype(jnp.bfloat16)
    grad_out_proj = contract(grad_mid_low, mixed_heads.reshape(seq_len, QD), 0, 0)
    grad_heads = contract(grad_mid_low, attn_weight[:, QD + 2 * KD :], 1, 0).astype(jnp.bfloat16)
    grad_heads = grad_heads.reshape(seq_len, KV_HEADS, GROUP, HEAD_DIM)
    grad_queries, grad_keys, grad_values = attend_back(
        kept_state["queries"],
        kept_state["key_rows"],
        kept_state["value_rows"],
        kept_state["allowed"],
        mixed_heads,
        kept_state["log_totals"],
        grad_heads,
    )
    cosine = kept_state["cosine"]
    sine_tab = kept_state["sine_tab"]
    grad_q_part = grad_queries.reshape(seq_len, HEADS, HEAD_DIM)
    grad_q_part = grad_q_part * cosine - rotate_half(grad_q_part) * sine_tab
    grad_k_part = grad_keys * cosine - rotate_half(grad_keys) * sine_tab
    grad_projected = jnp.concatenate(
        [
            grad_q_part.reshape(seq_len, QD),
            grad_k_part.reshape(seq_len, KD),
            grad_values.reshape(seq_len, KD),
        ],
        axis=1,
    ).astype(jnp.bfloat16)
    grad_qkv = contract(kept_state["input_one"], grad_projected, 0, 0)
    grad_input_one = contract(grad_projected, attn_weight[:, : QD + 2 * KD], 1, 1)
    grad_norm_one, grad_gain_one = norm_back(
        grad_input_one, kept_state["normed_one"], kept_state["inv_one"], norm_gains[:model_width]
    )
    grad_tokens = grad_middle + grad_norm_one
    grad_attn = jnp.concatenate([grad_qkv, grad_out_proj], axis=1)
    return (grad_tokens, grad_attn, grad_gain_one)


def device_rows(parts, devices):
    widths = [matrix.shape[dim] // devices for matrix, dim in parts]
    per_device = sum(widths)

    def term_rows(start, count):
        blocks_here = count // per_device
        blocks = []
        for (matrix, dim), width in zip(parts, widths):
            piece = matrix
            if dim == 1:
                piece = piece.T
            blocks.append(piece.reshape(blocks_here, width, piece.shape[1]))
        return jnp.concatenate(blocks, axis=1).reshape(blocks_here * per_device, -1)

    return (term_rows, widths, per_device)


def split_rows(summed, parts, widths):
    results = []
    offset = 0
    for (matrix, dim), width in zip(parts, widths):
        block = summed[offset : offset + width]
        results.append(block.T if dim == 1 else block)
        offset = offset + width
    return results


def on_device(
    tokens,
    out_grad,
    segment_ids,
    positions,
    attn_weight,
    gate_weight,
    up_weight,
    down_weight,
    norm_gains,
):
    devices = lax.axis_size("dp")
    gathered = (
        lax.all_gather(attn_weight, "dp", axis=1, tiled=True),
        lax.all_gather(gate_weight, "dp", axis=1, tiled=True),
        lax.all_gather(up_weight, "dp", axis=1, tiled=True),
        lax.all_gather(down_weight, "dp", axis=0, tiled=True),
        lax.all_gather(norm_gains, "dp", axis=0, tiled=True),
    )
    output, kept_state = layer_forward(
        tokens,
        segment_ids[0],
        positions[0],
        gathered[0],
        gathered[1],
        gathered[2],
        gathered[3],
        gathered[4],
    )
    grad_middle, grad_gain_two, ffn_grads = ffn_backward(
        out_grad, kept_state, gathered[1], gathered[2], gathered[3], gathered[4]
    )
    grad_tokens, grad_attn, grad_gain_one = attn_backward(
        grad_middle, kept_state, gathered[0], gathered[4]
    )
    grad_gains = jnp.concatenate([grad_gain_one, grad_gain_two])
    all_parts = [(grad_attn, 1), (ffn_grads[0], 1), (ffn_grads[1], 1), (ffn_grads[2], 0)]
    all_fn, all_widths, all_rows = device_rows(all_parts, devices)
    all_summed = lax.psum_scatter(
        all_fn(jnp.int32(0), all_rows * lax.axis_size("dp")), "dp", scatter_dimension=0, tiled=True
    )
    shares = tuple(split_rows(all_summed, all_parts, all_widths))
    gain_share = lax.psum_scatter(grad_gains, "dp", scatter_dimension=0, tiled=True)
    return (output, grad_tokens, shares[0], shares[1], shares[2], shares[3], gain_share)


def solution(mesh):
    in_specs = (
        P("dp", None),
        P("dp", None),
        P("dp", None),
        P("dp", None),
        P(None, "dp"),
        P(None, "dp"),
        P(None, "dp"),
        P("dp", None),
        P("dp"),
    )
    out_specs = (
        P("dp", None),
        P("dp", None),
        P(None, "dp"),
        P(None, "dp"),
        P(None, "dp"),
        P("dp", None),
        P("dp"),
    )
    return jax.shard_map(
        on_device, mesh=mesh, in_specs=in_specs, out_specs=out_specs, check_vma=False
    )
```

profile of v0, /device:TPU:8, one launch (start us, length us, event | category | flops | bytes accessed | tf_op | source)
XLA Modules:
  0.0 824.9 jit_solution(10276416389014661938)
XLA Ops:
  7.2 0.7 all-gather.5.cloned.1.call-update
  7.9 0.0 all-gather.9.cloned.1.call-start
  7.9 0.7 all-gather.9.cloned.1.call-update
  8.7 0.7 all-gather.7.cloned.1.call-update
  9.4 0.5 all-gather.11.cloned.1.call-update
  10.0 0.0 reduce-scatter.2.cloned.1.call-start
  10.0 0.7 convert_element_type.92
  10.7 0.8 dynamic-update-slice
  11.5 40.8 %all-reduce = bf16[1920]{0:T(1024)(128)(2,1)S(1)} all-reduce(bf16[1920]{0:T(1024)(128)(2,1)S(1)} %dynamic-update-slice), channel_id=1, replica_groups=mesh['dp'=32] {'dp'}, use_global_device_ids=true, to_apply=%add | all-reduce | flops 1920 | bytes 7680
  52.3 0.1 broadcast_multiply_fusion
  52.4 0.1 fusion.58
  52.5 1.2 fusion.40
  53.8 0.1 slice_convert_fusion.1
  53.8 0.9 fusion.50
  54.7 22.7 %all-gather.5.cloned.1.call-done = bf16[960,2560]{0,1:T(8,128)(2,1)} async-done(((bf16[960,80]{0,1:T(8,128)(2,1)}), bf16[960,2560]{0,1:T(8,128)(2,1)}) %all-gather.5.cloned.1.call-update) | async-done | bytes 4915216 | tf_op jit(solution)/shard_map/all_gather | solution.py:236
  77.4 3.1 fusion.7
  80.6 0.1 slice.87
  80.7 0.1 fusion.54
  80.8 0.1 slice_negate_fusion.1
  80.9 0.2 fusion.42
  81.1 0.8 fusion.62
  81.9 0.6 fusion.3
  82.5 0.8 fusion.24
  83.3 0.6 copy-done
  83.9 2.6 multiply_reduce_fusion.3
  86.6 0.2 multiply_convert_fusion.3
  86.8 57.3 %all-gather.9.cloned.1.call-done = bf16[960,2560]{0,1:T(8,128)(2,1)} async-done(((bf16[960,80]{0,1:T(8,128)(2,1)}), bf16[960,2560]{0,1:T(8,128)(2,1)}) %all-gather.9.cloned.1.call-update) | async-done | bytes 4915216 | tf_op jit(solution)/shard_map/all_gather | solution.py:238
  144.1 5.6 fusion.64
  149.7 61.1 %all-gather.7.cloned.1.call-done = bf16[960,2560]{0,1:T(8,128)(2,1)} async-done(((bf16[960,80]{0,1:T(8,128)(2,1)}), bf16[960,2560]{0,1:T(8,128)(2,1)}) %all-gather.7.cloned.1.call-update) | async-done | bytes 4915216 | tf_op jit(solution)/shard_map/all_gather | solution.py:237
  210.8 5.5 fusion.63
  216.3 61.0 %all-gather.11.cloned.1.call-done = bf16[2560,960]{1,0:T(8,128)(2,1)} async-done(((bf16[80,960]{1,0:T(8,128)(2,1)}), bf16[2560,960]{1,0:T(8,128)(2,1)}) %all-gather.11.cloned.1.call-update) | async-done | bytes 4915216 | tf_op jit(solution)/shard_map/all_gather | solution.py:239
  277.3 8.7 %multiply_convert_fusion = (bf16[256,2560]{1,0:T(8,128)(2,1)S(1)}, bf16[256,2560]{1,0:T(8,128)(2,1)S(1)}, bf16[256,2560]{1,0:T(8,128)(2,1)}) fusion(f32[256,2560]{1,0:T(8,128)} %fusion.63, f32[256,2560]{1,0:T(8,128)} %fusion.64, bf16[256,960]{0,1:T(8,128)(2,1)S(1)} %copy-done.3, bf16[2560,960]{1,0:T(8,128)(2,1)} %all-gather.11.cloned.1.call-done), kind=kOutput, calls=%fused_computation.16 | convolution fusion | flops 1268776960 | bytes 14581760 | tf_op jit(solution)/shard_map/dot_general | solution.py:24
  286.0 2.2 fusion.65
  288.2 4.9 multiply_reduce_fusion
  293.1 0.3 multiply_add_fusion
  293.5 2.4 fusion.25
  295.9 0.2 multiply_reduce_fusion.1
  296.0 0.7 fusion.31
  296.8 1.1 fusion.2
  298.0 0.7 convolution_bitcast_fusion
  298.7 0.5 fusion.66
  299.2 2.6 fusion.51
  301.8 5.5 fusion.68
  307.3 5.4 fusion.67
  312.7 0.1 slice_negate_fusion
  312.8 0.1 maximum_multiply_fusion.1
  312.9 0.2 fusion.44
  313.1 0.1 fusion.49
  313.2 0.6 copy-done.14
  313.8 4.0 fusion.45
  317.8 9.6 %maximum_bitcast_fusion = f32[2560,960]{0,1:T(8,128)} fusion(f32[960,960]{1,0:T(8,128)} %fusion.51, f32[960,1600]{1,0:T(8,128)} %fusion.45), kind=kLoop, calls=%fused_computation.1 | loop fusion | flops 2457600 | bytes 19660800 | tf_op jit(solution)/shard_map/transpose | solution.py:206
  327.4 11.3 %copy.33 = f32[2560,960]{1,0:T(8,128)} copy(f32[2560,960]{0,1:T(8,128)} %maximum_bitcast_fusion) | data formatting | bytes 19660800 | tf_op jit(solution)/shard_map/transpose | solution.py:206
  338.7 6.8 fusion.69
  345.5 28.4 %pad_maximum_fusion = f32[32,320,960]{2,1,0:T(8,128)} fusion(f32[32,80,960]{2,1,0:T(8,128)} %bitcast.106, f32[32,80,960]{2,1,0:T(8,128)} %bitcast.104, f32[32,80,960]{2,1,0:T(8,128)} %bitcast.105, f32[32,80,960]{2,1,0:T(8,128)} %bitcast.107), kind=kLoop, calls=%fused_computation | loop fusion | flops 29491200 | bytes 78643200 | tf_op jit(solution)/shard_map/concatenate | solution.py:208
  374.0 0.9 copy-done.15
  374.9 0.1 copy-done.17
  375.0 4.4 fusion.39
  379.4 0.1 pad_maximum_fusion.5
  379.4 58.3 %all-reduce.1 = f32[1920]{0:T(1024)S(1)} all-reduce(f32[1920]{0:T(1024)S(1)} %pad_maximum_fusion.5), channel_id=3, replica_groups=mesh['dp'=32] {'dp'}, use_global_device_ids=true, to_apply=%region_10.11.clone | all-reduce | flops 1920 | bytes 15360
  437.7 0.6 dynamic-slice
  438.3 2.4 fusion.38
  440.7 5.8 fusion.23
  446.5 369.5 %reduce-scatter.2.cloned.1.call-done = f32[320,960]{1,0:T(8,128)} async-done(((f32[10240,960]{1,0:T(8,128)}), f32[320,960]{1,0:T(8,128)}) %reduce-scatter.2.cloned.1.call-update) | async-done | bytes 1228816 | tf_op jit(solution)/shard_map/reduce_scatter | solution.py:261
  816.0 2.3 fusion.61
  (49 shorter events, 0.4 us)
Async XLA Ops:
  7.2 70.3 %all-gather.5.cloned.1.call-start = ((), (), s32[]{:S(2)}) async-start(), calls=%async_computation.1 | async-start | bytes 5406720 | tf_op jit(solution)/shard_map/all_gather | solution.py:236
  7.9 136.2 %all-gather.9.cloned.1.call-start = ((), (), s32[]{:S(2)}) async-start(), calls=%async_computation.3 | async-start | bytes 5406720 | tf_op jit(solution)/shard_map/all_gather | solution.py:238
  8.6 202.2 %all-gather.7.cloned.1.call-start = ((), (), s32[]{:S(2)}) async-start(), calls=%async_computation.2 | async-start | bytes 5406720 | tf_op jit(solution)/shard_map/all_gather | solution.py:237
  9.4 268.0 %all-gather.11.cloned.1.call-start = ((), (), s32[]{:S(2)}) async-start(), calls=%async_computation.4 | async-start | bytes 5406720 | tf_op jit(solution)/shard_map/all_gather | solution.py:239
  10.0 806.0 %reduce-scatter.2.cloned.1.call-start = ((), (), s32[]{:S(2)}) async-start(), calls=%async_computation.5 | async-start | bytes 43253760 | tf_op jit(solution)/shard_map/reduce_scatter | solution.py:261
  52.5 28.4 %copy-start.8 = (f32[256,64]{0,1:T(8,128)}, f32[256,64]{0,1:T(8,128)S(1)}, u32[]{:S(2)}) copy-start(f32[256,64]{0,1:T(8,128)S(1)} %get-tuple-element.27) | copy-start | bytes 196612
  80.6 1.9 copy-start.12
  80.8 1.1 copy-start.10
  81.9 2.0 copy-start
  82.5 1.4 copy-start.2
  83.9 2.7 copy-start.6
  149.7 127.7 %copy-start.3 = (bf16[256,960]{0,1:T(8,128)(2,1)S(1)}, bf16[256,960]{0,1:T(8,128)(2,1)}, u32[]{:S(2)}) copy-start(bf16[256,960]{0,1:T(8,128)(2,1)} %param.10) | copy-start | bytes 1474564
  277.3 8.7 %copy-start.18 = (bf16[960,2560]{0,1:T(8,128)(2,1)S(1)}, bf16[960,2560]{0,1:T(8,128)(2,1)}, u32[]{:S(2)}) copy-start(bf16[960,2560]{0,1:T(8,128)(2,1)} %all-gather.7.cloned.1.call-done) | copy-start | bytes 14745604
  288.2 4.9 copy-start.4
  293.1 2.8 copy-start.7
  293.1 2.9 copy-start.1
  293.4 3.4 copy-start.13
  296.8 16.4 %copy-start.16 = (bf16[5,64,256]{2,1,0:T(8,128)(2,1)}, bf16[5,64,256]{2,1,0:T(8,128)(2,1)S(1)}, u32[]{:S(2)}) copy-start(bf16[5,64,256]{2,1,0:T(8,128)(2,1)S(1)} %fusion.31) | copy-start | bytes 491524
  296.8 1.9 copy-start.11
  307.3 5.5 copy-start.9
  313.2 0.7 copy-start.14
  327.4 11.3 %copy-start.5 = (bf16[256,960]{0,1:T(8,128)(2,1)S(1)}, bf16[256,960]{0,1:T(8,128)(2,1)}, u32[]{:S(2)}) copy-start(bf16[256,960]{0,1:T(8,128)(2,1)} %param.10) | copy-start | bytes 1474564
  374.0 0.9 copy-start.15
  374.0 1.0 copy-start.17
Sparse Core Ops, SparseCore 0:
  10.8 66.5 all-gather.4
  80.3 63.7 all-gather.8
  147.0 63.7 all-gather.6
  213.5 63.7 all-gather.10
  374.1 441.8 reduce-scatter.1
where the time goes:
time: 833 us; the launch traced here: 825 us
  waiting for transfers between devices  574 us (69%)
  blocking collectives  99 us (12%)
  matrix products  74.2 us (9%)
  other arithmetic  45.6 us (5%)
  local copies, waits for them, and re-layouts  17.4 us (2%)
  between operations  14.2 us (2%)
    reduce_scatter x1, waiting for transfers between devices, on_device(): lax.psum_scatter(all_fn(jnp.int32(0), all_rows * lax.axis_size('dp')), 'd...  369 us
    unnamed x2, blocking collectives  99 us
    dot_general x15, matrix products, contract(): lax.dot_general(left, right, (((left_axis,), (right_axis,)), ((), ())), p...  69.6 us
    all_gather x1, waiting for transfers between devices, on_device(): lax.all_gather(gate_weight, 'dp', axis=1, tiled=True)  61.1 us
    all_gather x1, waiting for transfers between devices, on_device(): lax.all_gather(down_weight, 'dp', axis=0, tiled=True)  61 us
    all_gather x1, waiting for transfers between devices, on_device(): lax.all_gather(up_weight, 'dp', axis=1, tiled=True)  57.3 us
    concatenate x1, other arithmetic, term_rows(): return jnp.concatenate(blocks, axis=1).reshape(blocks_here * per_device, -1)  28.4 us
    all_gather x1, waiting for transfers between devices, on_device(): lax.all_gather(attn_weight, 'dp', axis=1, tiled=True)  22.7 us
  transfers between devices with their start and end apart: 5, of which 5 were waited for; matrix products, arithmetic and copies ran while one was open for 4% of the time, Pallas kernels for 0%

commit v1 on v0

--- a/solution.py
+++ b/solution.py
@@ -1,6 +1,8 @@
 import jax
 import jax.numpy as jnp
 from jax import lax
+from jax.experimental import pallas as pl
+from jax.experimental.pallas import tpu as pltpu
 from jax.sharding import PartitionSpec as P
 
 HEADS = 15
@@ -87,13 +89,13 @@
 
 
 def layer_forward(
-    tokens, segments, positions, attn_weight, gate_weight, up_weight, down_weight, norm_gains
+    tokens, segments, positions, attn_rows, gate_rows, up_rows, down_weight, norm_gains
 ):
     seq_len = tokens.shape[0]
     model_width = tokens.shape[1]
     residual = tokens.astype(jnp.float32)
     normed_one, inv_one, input_one = norm_rows(residual, norm_gains[:model_width])
-    projected = contract(input_one, attn_weight[:, : QD + 2 * KD], 1, 0)
+    projected = contract(input_one, attn_rows[: QD + 2 * KD], 1, 1)
     cosine, sine_tab = rope_tables(positions)
     query_part = projected[:, :QD].reshape(seq_len, HEADS, HEAD_DIM)
     key_part = projected[:, QD : QD + KD].reshape(seq_len, KV_HEADS, HEAD_DIM)
@@ -104,10 +106,10 @@
     allowed = allowed_pairs(segments)
     mixed_heads, log_totals = attend(queries, key_rows, value_rows, allowed)
     mixed_flat = mixed_heads.reshape(seq_len, QD)
-    middle = residual + contract(mixed_flat, attn_weight[:, QD + 2 * KD :], 1, 1)
+    middle = residual + contract(mixed_flat, attn_rows[QD + 2 * KD :], 1, 0)
     normed_two, inv_two, input_two = norm_rows(middle, norm_gains[model_width:])
-    gate_act = contract(input_two, gate_weight, 1, 0)
-    up_proj = contract(input_two, up_weight, 1, 0)
+    gate_act = contract(input_two, gate_rows, 1, 1)
+    up_proj = contract(input_two, up_rows, 1, 1)
     hidden = (jax.nn.silu(gate_act) * up_proj).astype(jnp.bfloat16)
     output = middle + contract(hidden, down_weight, 1, 0)
     kept_state = {
@@ -132,7 +134,7 @@
     return (output.astype(jnp.bfloat16), kept_state)
 
 
-def ffn_backward(out_grad, kept_state, gate_weight, up_weight, down_weight, norm_gains):
+def ffn_backward(out_grad, kept_state, gate_rows, up_rows, down_weight, norm_gains):
     model_width = out_grad.shape[1]
     gate_act = kept_state["gate_act"]
     input_two = kept_state["input_two"]
@@ -143,9 +145,9 @@
         grad_hidden * kept_state["up_proj"] * sig_gate * (1.0 + gate_act * (1.0 - sig_gate))
     ).astype(jnp.bfloat16)
     grad_up = (grad_hidden * gate_act * sig_gate).astype(jnp.bfloat16)
-    grad_gate_w = contract(input_two, grad_gate, 0, 0)
-    grad_up_w = contract(input_two, grad_up, 0, 0)
-    grad_input_two = contract(grad_gate, gate_weight, 1, 1) + contract(grad_up, up_weight, 1, 1)
+    grad_gate_w = contract(grad_gate, input_two, 0, 0)
+    grad_up_w = contract(grad_up, input_two, 0, 0)
+    grad_input_two = contract(grad_gate, gate_rows, 1, 0) + contract(grad_up, up_rows, 1, 0)
     grad_norm_two, grad_gain_two = norm_back(
         grad_input_two, kept_state["normed_two"], kept_state["inv_two"], norm_gains[model_width:]
     )
@@ -153,13 +155,13 @@
     return (grad_middle, grad_gain_two, (grad_gate_w, grad_up_w, grad_down))
 
 
-def attn_backward(grad_middle, kept_state, attn_weight, norm_gains):
+def attn_backward(grad_middle, kept_state, attn_rows, norm_gains):
     seq_len = grad_middle.shape[0]
     model_width = grad_middle.shape[1]
     mixed_heads = kept_state["mixed_heads"]
     grad_mid_low = grad_middle.astype(jnp.bfloat16)
-    grad_out_proj = contract(grad_mid_low, mixed_heads.reshape(seq_len, QD), 0, 0)
-    grad_heads = contract(grad_mid_low, attn_weight[:, QD + 2 * KD :], 1, 0).astype(jnp.bfloat16)
+    grad_out_proj = contract(mixed_heads.reshape(seq_len, QD), grad_mid_low, 0, 0)
+    grad_heads = contract(grad_mid_low, attn_rows[QD + 2 * KD :], 1, 1).astype(jnp.bfloat16)
     grad_heads = grad_heads.reshape(seq_len, KV_HEADS, GROUP, HEAD_DIM)
     grad_queries, grad_keys, grad_values = attend_back(
         kept_state["queries"],
@@ -183,41 +185,444 @@
         ],
         axis=1,
     ).astype(jnp.bfloat16)
-    grad_qkv = contract(kept_state["input_one"], grad_projected, 0, 0)
-    grad_input_one = contract(grad_projected, attn_weight[:, : QD + 2 * KD], 1, 1)
+    grad_qkv = contract(grad_projected, kept_state["input_one"], 0, 0)
+    grad_input_one = contract(grad_projected, attn_rows[: QD + 2 * KD], 1, 0)
     grad_norm_one, grad_gain_one = norm_back(
         grad_input_one, kept_state["normed_one"], kept_state["inv_one"], norm_gains[:model_width]
     )
     grad_tokens = grad_middle + grad_norm_one
-    grad_attn = jnp.concatenate([grad_qkv, grad_out_proj], axis=1)
+    grad_attn = jnp.concatenate([grad_qkv.astype(jnp.bfloat16), grad_out_proj.astype(jnp.bfloat16)], axis=0)
     return (grad_tokens, grad_attn, grad_gain_one)
 
 
-def device_rows(parts, devices):
-    widths = [matrix.shape[dim] // devices for matrix, dim in parts]
-    per_device = sum(widths)
-
-    def term_rows(start, count):
-        blocks_here = count // per_device
-        blocks = []
-        for (matrix, dim), width in zip(parts, widths):
-            piece = matrix
-            if dim == 1:
-                piece = piece.T
-            blocks.append(piece.reshape(blocks_here, width, piece.shape[1]))
-        return jnp.concatenate(blocks, axis=1).reshape(blocks_here * per_device, -1)
-
-    return (term_rows, widths, per_device)
-
-
-def split_rows(summed, parts, widths):
-    results = []
-    offset = 0
-    for (matrix, dim), width in zip(parts, widths):
-        block = summed[offset : offset + width]
-        results.append(block.T if dim == 1 else block)
-        offset = offset + width
-    return results
+MESH = pl.DeviceIdType.MESH
+AXES = ("z", "y", "x")
+SIZES = {"z": 4, "y": 2, "x": 2}
+STRIDES = {"z": 8, "y": 4, "x": 2}
+gather_orders = ("xyz", "yxz", "zxy", "zyx", "zxy", "zyx", "zxy", "zyx")
+
+
+def gather_parts(rows):
+    first = (rows // 2 + 15) // 16 * 16
+    halves = [(0, first), (first, rows - first)]
+    parts = []
+    for weight in range(4):
+        for half, (start, count) in enumerate(halves):
+            parts.append((weight, start, count, gather_orders[2 * weight + half]))
+    return parts
+
+
+def place():
+    me = lax.axis_index("dp")
+    return {
+        "me": me,
+        "core": lax.rem(me, 2),
+        "x": lax.rem(me // 2, 2),
+        "y": lax.rem(me // 4, 2),
+        "z": me // 8,
+    }
+
+
+def neighbours(at):
+    me = at["me"]
+    found = {
+        "core": me + 1 - 2 * at["core"],
+        "x": me + 2 - 4 * at["x"],
+        "y": me + 4 - 8 * at["y"],
+        "up": lax.rem(me + 8, 32),
+        "down": lax.rem(me + 24, 32),
+    }
+    return found
+
+
+def greet(near):
+    barrier = pltpu.get_barrier_semaphore()
+    for device in near.values():
+        pl.semaphore_signal(barrier, inc=1, device_id=(device,), device_id_type=MESH)
+    pl.semaphore_wait(barrier, len(near))
+
+
+def arrival_order(parts, weights, reverse):
+    free = {"z": 0.0, "y": 0.0, "x": 0.0, "core": 0.0}
+    jobs, order, tick = [], [], 0
+
+    def push(ready, link, size, part, phase, step):
+        nonlocal tick
+        tick += 1
+        jobs.append((ready, tick, link, size, part, phase, step))
+
+    def phase_size(order_of, phase):
+        size = 1.0
+        for axis in order_of[:phase]:
+            size *= SIZES[axis]
+        return size
+
+    def begin(part, phase, ready):
+        axes = parts[part][3]
+        if phase < 3:
+            rank = 2 - phase if reverse else phase
+            link = axes[rank]
+            push(ready, link, weights[part] * phase_size(axes, rank), part, phase, 0)
+
+    for part in range(len(parts)):
+        if reverse:
+            push(0.0, "core", weights[part] * 16 / 6, part, -1, 0)
+        else:
+            begin(part, 0, 0.0)
+    while jobs:
+        job = min(jobs, key=lambda item: (max(item[0], free[item[2]]), item[1]))
+        jobs.remove(job)
+        ready, _, link, size, part, phase, step = job
+        end = max(ready, free[link]) + size
+        free[link] = end
+        order.append((end, part, phase, step))
+        if link == "z" and step < 2:
+            push(end, link, size, part, phase, step + 1)
+        else:
+            begin(part, phase + 1, end)
+    order.sort()
+    return [(part, phase, step) for _, part, phase, step in order]
+
+
+class Copies:
+    def __init__(self, send_sems, recv_sems):
+        self.send_sems, self.recv_sems = send_sems, recv_sems
+        self.slots, self.pending = {}, []
+
+    def slot(self, key):
+        return self.slots.setdefault(key, len(self.slots))
+
+    def copy(self, key, source, target, device):
+        index = self.slot(key)
+        return pltpu.make_async_remote_copy(
+            src_ref=source,
+            dst_ref=target,
+            send_sem=self.send_sems.at[index],
+            recv_sem=self.recv_sems.at[index],
+            device_id=(device,),
+            device_id_type=MESH,
+        )
+
+    def start(self, key, source, target, device, when=None):
+        copy = self.copy(key, source(), target(), device)
+        run, finish = copy.start, copy.wait_send
+
+        if when is None:
+            run()
+            self.pending.append(finish)
+        else:
+            pl.when(when)(lambda: run())
+            self.pending.append(lambda: pl.when(when)(lambda: finish()))
+
+    def arrive(self, key, target, device):
+        self.copy(key, target, target, device).wait_recv()
+
+    def drain(self):
+        for finish in self.pending:
+            finish()
+
+
+def gather_kernel(parts, events, *refs):
+    count = 5
+    ins, outs = refs[:count], refs[count : 2 * count]
+    send_sems, recv_sems, local_sems = refs[2 * count :]
+    at = place()
+    near = neighbours(at)
+    z = at["z"]
+    copies = Copies(send_sems, recv_sems)
+    locals_ = []
+    for which in range(count):
+        own = outs[which].at[pl.ds(z, 1), pl.ds(at["y"], 1), pl.ds(at["x"], 1), pl.ds(at["core"], 1)]
+        local = pltpu.make_async_copy(ins[which], own, local_sems.at[which])
+        local.start()
+        locals_.append(local)
+    greet(near)
+    for local in locals_:
+        local.wait()
+
+    def view(part, chosen, core=None):
+        weight, start, rows, _ = parts[part]
+        index = []
+        for axis in AXES:
+            index.append(pl.ds(chosen[axis], 1) if axis in chosen else slice(None))
+        index.append(pl.ds(at["core"] if core is None else core, 1))
+        return outs[weight].at[tuple(index) + (pl.ds(start, rows),)]
+
+    def fixed(part, phase):
+        return {axis: at[axis] for axis in parts[part][3][phase + 1 :]}
+
+    core_arrivals = []
+
+    def to_partner(part, tag, chosen, when=None):
+        key = (part, "core", tag)
+        copies.start(
+            key, lambda: view(part, chosen()), lambda: view(part, chosen()), near["core"], when
+        )
+
+        def land():
+            copies.arrive(key, view(part, chosen(), 1 - at["core"]), near["core"])
+
+        core_arrivals.append(land if when is None else (lambda: pl.when(when)(land)))
+
+    def begin(part, phase):
+        axis = parts[part][3][phase]
+        chosen = dict(fixed(part, phase), **{axis: at[axis]})
+        block = lambda: view(part, chosen)
+        if axis == "z":
+            copies.start((part, "up", 1), block, block, near["up"], z < 3)
+            copies.start((part, "down", 1), block, block, near["down"], z > 0)
+        else:
+            copies.start((part, axis), block, block, near[axis])
+
+    for part in range(len(parts)):
+        begin(part, 0)
+    for part in range(len(parts)):
+        to_partner(part, "own", lambda: {axis: at[axis] for axis in AXES})
+
+    for part, phase, step in events:
+        axis = parts[part][3][phase]
+        rest = fixed(part, phase)
+        if axis == "z":
+            hop = step + 1
+            for way, sign, onward in (("up", -1, z < 3), ("down", 1, z > 0)):
+                there = (z >= hop) if sign < 0 else (z + hop <= 3)
+                chosen = lambda rest=rest, sign=sign, hop=hop: dict(rest, z=z + sign * hop)
+
+                @pl.when(there)
+                def _(way=way, chosen=chosen, hop=hop):
+                    copies.arrive((part, way, hop), view(part, chosen()), near[way])
+
+                if hop < 3:
+                    block = lambda part=part, chosen=chosen: view(part, chosen())
+                    copies.start(
+                        (part, way, hop + 1), block, block, near[way], jnp.logical_and(there, onward)
+                    )
+                to_partner(part, (way, hop), chosen, there)
+        else:
+            chosen = dict(rest, **{axis: 1 - at[axis]})
+            copies.arrive((part, axis), view(part, chosen), near[axis])
+            to_partner(part, axis, lambda chosen=chosen: chosen)
+        if (axis != "z" or step == 2) and phase < 2:
+            begin(part, phase + 1)
+    for land in core_arrivals:
+        land()
+    copies.drain()
+
+
+def sized_parts(shapes):
+    rows = shapes[0][-2]
+    parts = gather_parts(rows) + [(4, 0, shapes[4][-2], "zxy")]
+    weights = [part[2] * shapes[part[0]][-1] / (rows * shapes[0][-1]) for part in parts]
+    return parts, weights
+
+
+def gather_all(blocks):
+    shapes = [block.shape for block in blocks]
+    parts, weights = sized_parts(shapes)
+    events = arrival_order(parts, weights, False)
+    return pl.pallas_call(
+        lambda *refs: gather_kernel(parts, events, *refs),
+        out_shape=[
+            jax.ShapeDtypeStruct((4, 2, 2, 2) + shape[4:], block.dtype)
+            for shape, block in zip(shapes, blocks)
+        ],
+        in_specs=[pl.BlockSpec(memory_space=pltpu.VMEM)] * 5,
+        out_specs=[pl.BlockSpec(memory_space=pl.ANY)] * 5,
+        scratch_shapes=[
+            pltpu.SemaphoreType.DMA((len(parts) * 18,)),
+            pltpu.SemaphoreType.DMA((len(parts) * 18,)),
+            pltpu.SemaphoreType.DMA((5,)),
+        ],
+        compiler_params=pltpu.CompilerParams(collective_id=0, has_side_effects=True),
+        name="gather_all",
+    )(*blocks)
+
+
+def scatter_kernel(parts, events, buffers, *refs):
+    count = 5
+    grads, outs = refs[:count], refs[count : 2 * count]
+    refs = refs[2 * count :]
+    sums, landed = refs[:count], refs[count : 2 * count]
+    refs = refs[2 * count :]
+    bufs = dict(zip(buffers, refs[: len(buffers)]))
+    send_sems, recv_sems, local_sems = refs[len(buffers) :]
+    at = place()
+    near = neighbours(at)
+    z = at["z"]
+    core = at["core"]
+    copies = Copies(send_sems, recv_sems)
+
+    def rows_of(part):
+        return pl.ds(parts[part][1], parts[part][2])
+
+    locals_ = []
+    for part, (weight, *_) in enumerate(parts):
+        local = pltpu.make_async_copy(
+            grads[weight].at[:, :, :, pl.ds(core, 1), rows_of(part)],
+            sums[weight].at[:, :, :, :, rows_of(part)],
+            local_sems.at[part],
+        )
+        local.start()
+        locals_.append(local)
+    greet(near)
+
+    def phases(part):
+        return parts[part][3][::-1]
+
+    def add_block(part, chosen, source, source_rows):
+        weight, start, rows, _ = parts[part]
+        target = sums[weight]
+        spans = [1 if axis in chosen else SIZES[axis] for axis in AXES]
+        bases = [chosen.get(axis, 0) for axis in AXES]
+
+        def body(step, carry):
+            k = step % spans[2]
+            j = (step // spans[2]) % spans[1]
+            i = step // (spans[2] * spans[1])
+            there = (i + bases[0], j + bases[1], k + bases[2], 0, pl.ds(start, rows))
+            target[there] = target[there] + source[i, j, k, 0, source_rows]
+            return carry
+
+        lax.fori_loop(0, spans[0] * spans[1] * spans[2], body, 0)
+
+    def begin(part, phase):
+        axis = phases(part)[phase]
+        before = {name: at[name] for name in phases(part)[:phase]}
+        weight = parts[part][0]
+        target = lambda slot: bufs[(part, phase, slot)]
+        if axis == "z":
+            for j in range(3):
+                block = lambda q, before=before: view(part, dict(before, z=q))
+                copies.start((part, "up", j), lambda j=j: block(3 - j), lambda j=j: target(("up", j)), near["up"], z == 0)
+                copies.start((part, "down", j), lambda j=j: block(j), lambda j=j: target(("down", j)), near["down"], z == 3)
+        else:
+            chosen = dict(before, **{axis: 1 - at[axis]})
+            copies.start((part, axis), lambda: view(part, chosen), lambda: target(axis), near[axis])
+
+    def view(part, chosen):
+        index = []
+        for axis in AXES:
+            index.append(pl.ds(chosen[axis], 1) if axis in chosen else slice(None))
+        return sums[parts[part][0]].at[tuple(index) + (slice(None), rows_of(part))]
+
+    for part, (weight, *_) in enumerate(parts):
+        source = lambda weight=weight, part=part: grads[weight].at[
+            :, :, :, pl.ds(1 - core, 1), rows_of(part)
+        ]
+        target = lambda weight=weight, part=part: landed[weight].at[:, :, :, :, rows_of(part)]
+        copies.start((part, "core"), source, target, near["core"])
+
+    for part, phase, step in events:
+        weight, start, rows, _ = parts[part]
+        if phase < 0:
+            locals_[part].wait()
+            copies.arrive((part, "core"), landed[weight].at[:, :, :, :, rows_of(part)], near["core"])
+            add_block(part, {}, landed[weight], rows_of(part))
+            begin(part, 0)
+            continue
+        axis = phases(part)[phase]
+        before = {name: at[name] for name in phases(part)[:phase]}
+        if axis == "z":
+            j = step
+            ways = (
+                ("up", 3 - j, (z > 0) & (j <= 3 - z), (z > 0) & (z < 3) & (j <= 2 - z)),
+                ("down", j, (z < 3) & (j <= z), (z < 3) & (z > 0) & (j <= z - 1)),
+            )
+            for way, q, arrives, onward in ways:
+                buf = bufs[(part, phase, (way, j))]
+
+                @pl.when(arrives)
+                def _(way=way, q=q, buf=buf):
+                    copies.arrive((part, way, j), buf, near[way])
+                    add_block(part, dict(before, z=q), buf, slice(None))
+
+                copies.start(
+                    (part, way, j),
+                    lambda q=q: view(part, dict(before, z=q)),
+                    lambda buf=buf: buf,
+                    near[way],
+                    onward,
+                )
+        else:
+            buf = bufs[(part, phase, axis)]
+            copies.arrive((part, axis), buf, near[axis])
+            add_block(part, dict(before, **{axis: at[axis]}), buf, slice(None))
+        if axis != "z" or step == 2:
+            if phase < 2:
+                begin(part, phase + 1)
+            else:
+                outs[weight][rows_of(part), :] = sums[weight][
+                    at["z"], at["y"], at["x"], 0, rows_of(part)
+                ].astype(jnp.float32)
+    copies.drain()
+
+
+def scatter_all(grads):
+    shapes = [grad.shape for grad in grads]
+    parts, weights = sized_parts(shapes)
+    events = arrival_order(parts, weights, True)
+    buffers, shapes_of = [], []
+    for part, (weight, start, rows, order) in enumerate(parts):
+        extent = dict(SIZES)
+        for phase, axis in enumerate(order[::-1]):
+            extent[axis] = 1
+            shape = tuple(extent[name] for name in AXES) + (1, rows, shapes[weight][-1])
+            names = [(way, j) for way in ("up", "down") for j in range(3)] if axis == "z" else [axis]
+            for name in names:
+                buffers.append((part, phase, name))
+                shapes_of.append(pltpu.VMEM(shape, grads[weight].dtype))
+    plane = [pltpu.VMEM((4, 2, 2, 1) + shape[4:], grad.dtype) for shape, grad in zip(shapes, grads)]
+    return pl.pallas_call(
+        lambda *refs: scatter_kernel(parts, events, buffers, *refs),
+        out_shape=[jax.ShapeDtypeStruct(shape[4:], jnp.float32) for shape in shapes],
+        in_specs=[pl.BlockSpec(memory_space=pl.ANY)] * 5,
+        out_specs=[pl.BlockSpec(memory_space=pltpu.VMEM)] * 5,
+        scratch_shapes=plane
+        + plane
+        + shapes_of
+        + [
+            pltpu.SemaphoreType.DMA((len(parts) * 10,)),
+            pltpu.SemaphoreType.DMA((len(parts) * 10,)),
+            pltpu.SemaphoreType.DMA((len(parts),)),
+        ],
+        compiler_params=pltpu.CompilerParams(
+            collective_id=1, has_side_effects=True, vmem_limit_bytes=56 << 20
+        ),
+        name="scatter_all",
+    )(*grads)
+
+
+def gather_weights(shards, gains):
+    devices = lax.axis_size("dp")
+    rows, width = shards[0].shape
+    if devices == 32 and rows % 16 == 0:
+        gain_block = jnp.pad(gains[None, :], ((0, 15), (0, 128 - gains.shape[0])))
+        blocks = [block[None, None, None, None] for block in list(shards) + [gain_block]]
+        full = gather_all(blocks)
+        gathered = [block.reshape(devices * rows, width) for block in full[:4]]
+        return gathered, full[4].reshape(devices, 16, 128)[:, 0, : gains.shape[0]].reshape(-1)
+    gathered = [lax.all_gather(shard, "dp", axis=0, tiled=True) for shard in shards]
+    return gathered, lax.all_gather(gains, "dp", axis=0, tiled=True)
+
+
+def scatter_grads(grads, gain_grads):
+    devices = lax.axis_size("dp")
+    rows = grads[0].shape[0] // devices
+    width = grads[0].shape[1]
+    low = [grad.astype(jnp.bfloat16) for grad in grads]
+    gain_count = gain_grads.shape[0] // devices
+    if devices == 32 and rows % 16 == 0:
+        gain_block = jnp.pad(
+            gain_grads.reshape(devices, 1, gain_count), ((0, 0), (0, 7), (0, 128 - gain_count))
+        )
+        blocks = [grad.reshape(4, 2, 2, 2, rows, width) for grad in low]
+        shares = scatter_all(blocks + [gain_block.reshape(4, 2, 2, 2, 8, 128)])
+        return shares[:4], shares[4][0, :gain_count]
+    shares = [
+        lax.psum_scatter(grad, "dp", scatter_dimension=0, tiled=True).astype(jnp.float32)
+        for grad in low
+    ]
+    return shares, lax.psum_scatter(gain_grads, "dp", scatter_dimension=0, tiled=True)
 
 
 def on_device(
@@ -231,39 +636,29 @@
     down_weight,
     norm_gains,
 ):
-    devices = lax.axis_size("dp")
-    gathered = (
-        lax.all_gather(attn_weight, "dp", axis=1, tiled=True),
-        lax.all_gather(gate_weight, "dp", axis=1, tiled=True),
-        lax.all_gather(up_weight, "dp", axis=1, tiled=True),
-        lax.all_gather(down_weight, "dp", axis=0, tiled=True),
-        lax.all_gather(norm_gains, "dp", axis=0, tiled=True),
+    (attn_rows, gate_rows, up_rows, down_rows), gains = gather_weights(
+        (attn_weight.T, gate_weight.T, up_weight.T, down_weight), norm_gains
     )
     output, kept_state = layer_forward(
-        tokens,
-        segment_ids[0],
-        positions[0],
-        gathered[0],
-        gathered[1],
-        gathered[2],
-        gathered[3],
-        gathered[4],
+        tokens, segment_ids[0], positions[0], attn_rows, gate_rows, up_rows, down_rows, gains
     )
     grad_middle, grad_gain_two, ffn_grads = ffn_backward(
-        out_grad, kept_state, gathered[1], gathered[2], gathered[3], gathered[4]
+        out_grad, kept_state, gate_rows, up_rows, down_rows, gains
     )
     grad_tokens, grad_attn, grad_gain_one = attn_backward(
-        grad_middle, kept_state, gathered[0], gathered[4]
+        grad_middle, kept_state, attn_rows, gains
     )
     grad_gains = jnp.concatenate([grad_gain_one, grad_gain_two])
-    all_parts = [(grad_attn, 1), (ffn_grads[0], 1), (ffn_grads[1], 1), (ffn_grads[2], 0)]
-    all_fn, all_widths, all_rows = device_rows(all_parts, devices)
-    all_summed = lax.psum_scatter(
-        all_fn(jnp.int32(0), all_rows * lax.axis_size("dp")), "dp", scatter_dimension=0, tiled=True
-    )
-    shares = tuple(split_rows(all_summed, all_parts, all_widths))
-    gain_share = lax.psum_scatter(grad_gains, "dp", scatter_dimension=0, tiled=True)
-    return (output, grad_tokens, shares[0], shares[1], shares[2], shares[3], gain_share)
+    shares, gain_share = scatter_grads((grad_attn,) + ffn_grads, grad_gains)
+    return (
+        output,
+        grad_tokens,
+        shares[0].T,
+        shares[1].T,
+        shares[2].T,
+        shares[3],
+        gain_share,
+    )
 
 
 def solution(mesh):

time: 833 us -> 411 us (0.49)
  waiting for transfers between devices: 574 us -> 0 us
  Pallas kernels: 0 us -> 303 us
  blocking collectives: 99 us -> 0 us
  other arithmetic: 45.6 us -> 12.6 us
  local copies, waits for them, and re-layouts: 17.4 us -> 45.8 us
  matrix products: 74.2 us -> 47.3 us
  between operations: 14.2 us -> 1.17 us
    reduce_scatter x1 -> x0, waiting for transfers between devices: 369 us -> none  [on_device(): lax.psum_scatter(all_fn(jnp.int32(0), all_rows * lax.axis_size('dp')), 'd...]
    pallas_call x0 -> x2, Pallas kernels: none -> 303 us  [the longest x1 185 us: scatter_all(): pl.pallas_call(lambda *refs: scatter_kernel(parts, events, buffers, *refs...]
    all_gather x4 -> x0, waiting for transfers between devices: 202 us -> none  [the longest x1 61.1 us: on_device(): lax.all_gather(gate_weight, 'dp', axis=1, tiled=True)]
    unnamed x2 -> x0, blocking collectives: 99 us -> none
    dot_general x15, matrix products: 69.6 us -> 42.6 us  [contract(): lax.dot_general(left, right, (((left_axis,), (right_axis,)), ((), ())), p...]
    concatenate x1, other arithmetic: 28.4 us -> 3.59 us  [attn_backward(): jnp.concatenate([grad_qkv.astype(jnp.bfloat16), grad_out_proj.astype(jnp....]
    convert_element_type x0 -> x5, local copies, waits for them, and re-layouts: none -> 23.8 us  [the longest x3 23.7 us: scatter_grads(): low = [grad.astype(jnp.bfloat16) for grad in grads]]
    transpose x1 -> x0, local copies, waits for them, and re-layouts: 11.3 us -> none  [term_rows(): piece = piece.T]
  transfers between devices with their start and end apart: 5 -> 0, of which waited for: 5 -> 0; matrix products, arithmetic and copies ran while one was open for 4% -> 0% of each run, Pallas kernels for 0% -> 0%
where the time goes in v1:
time: 411 us; the launch traced here: 409 us
  Pallas kernels  303 us (74%)
  matrix products  47.3 us (12%)
  local copies, waits for them, and re-layouts  45.8 us (11%)
  other arithmetic  12.6 us (3%)
    pallas_call x1, Pallas kernels, scatter_all(): pl.pallas_call(lambda *refs: scatter_kernel(parts, events, buffers, *refs...  185 us
    pallas_call x1, Pallas kernels, gather_all(): pl.pallas_call(lambda *refs: gather_kernel(parts, events, *refs), out_sha...  118 us
    dot_general x15, matrix products, contract(): lax.dot_general(left, right, (((left_axis,), (right_axis,)), ((), ())), p...  42.6 us
    convert_element_type x3, local copies, waits for them, and re-layouts, scatter_grads(): low = [grad.astype(jnp.bfloat16) for grad in grads]  23.7 us
    unnamed x56, local copies, waits for them, and re-layouts  11.3 us

profile of v1, /device:TPU:8, one launch (start us, length us, event | category | flops | bytes accessed | tf_op | source)
XLA Modules:
  0.0 409.5 jit_solution(6972051120618513478)
XLA Ops:
  0.6 0.7 convert_element_type.126
  1.3 1.2 fusion.40
  2.5 1.3 pad_bitcast_fusion.refs_4_
  3.8 0.1 broadcast_multiply_fusion
  3.9 0.9 fusion.49
  4.7 0.1 fusion.56
  4.9 117.8 %gather_all.1 = (bf16[4,2,2,2,80,960]{5,4,3,2,1,0:T(8,128)(2,1)}, bf16[4,2,2,2,80,960]{5,4,3,2,1,0:T(8,128)(2,1)}, bf16[4,2,2,2,80,960]{5,4,3,2,1,0:T(8,128)(2,1...) custom-call(bf16[1,1,1,1,80,960]{5,4,3,2,1,0:T(8,128)(2,1)} %bitcast.146, ...), custom_call_target="tpu_custom_call" | custom-call | tf_op jit(solution)/shard_map/gather_all/pallas_call | solution.py:423
  122.6 0.8 fusion.57
  123.5 0.1 reshape.263
  123.5 0.1 reshape.262
  123.6 3.2 fusion.7
  126.9 0.1 slice.80
  127.0 0.1 fusion.52
  127.0 0.1 slice_negate_fusion.1
  127.2 0.2 fusion.42
  127.4 0.8 fusion.61
  128.2 0.6 fusion.3
  128.8 0.8 fusion.24
  129.6 0.6 copy-done
  130.1 1.6 copy-done.4
  131.7 2.5 multiply_reduce_fusion.3
  134.2 0.2 multiply_convert_fusion.3
  134.5 1.6 fusion.63
  136.1 0.3 slice-done.4
  136.4 0.4 slice-done.5
  136.7 3.2 fusion.62
  139.9 4.5 %multiply_convert_fusion = (bf16[256,2560]{1,0:T(8,128)(2,1)S(1)}, bf16[256,2560]{1,0:T(8,128)(2,1)S(1)}, bf16[256,2560]{1,0:T(8,128)(2,1)S(1)}) fusion(f32[256,2560]{1,0:T(8,128)} %fusion.62, f32[256,2560]{1,0:T(8,128)S(1)} %fusion.63, bf16[2560,960]{1,0:T(8,128)(2,1)S(1)} %bitcast.171, bf16[256,960]{0,1:T(8,128)(2,1)S(1)} %copy-done.2), kind=kOutput, calls=%fused_computation.20 | convolution fusion | flops 1268776960 | bytes 14581760 | tf_op jit(solution)/shard_map/dot_general | solution.py:26
  144.4 3.0 fusion.23
  147.4 2.2 fusion.64
  149.6 2.3 multiply_reduce_fusion
  151.9 0.3 multiply_add_fusion
  152.2 0.1 concatenate.53
  152.3 2.4 fusion.25
  154.7 1.2 multiply_reduce_fusion.1
  156.0 0.7 fusion.31
  156.8 1.1 fusion.2
  157.9 0.7 convolution_bitcast_fusion.1
  158.7 0.5 fusion.65
  159.2 0.1 fusion.48
  159.2 0.1 slice_negate_fusion
  159.3 0.1 maximum_multiply_fusion.1
  159.4 0.2 fusion.44
  159.6 1.3 slice-done.3
  160.9 0.2 copy-done.5
  161.1 1.7 fusion.39
  162.8 1.2 fusion.38
  164.1 0.1 concatenate.52
  164.1 0.9 select_maximum_fusion
  165.0 1.7 convolution_convert_fusion.4
  166.8 2.2 convolution_convert_fusion.3
  169.0 3.6 pad_maximum_fusion
  172.6 7.9 %copy.21 = bf16[2560,960]{1,0:T(8,128)(2,1)} copy(bf16[2560,960]{0,1:T(8,128)(2,1)} %pad_maximum_fusion) | data formatting | bytes 9830400 | tf_op jit(solution)/shard_map/concatenate | solution.py:194
  180.5 5.0 %convolution_convert_fusion = bf16[2560,960]{0,1:T(8,128)(2,1)} fusion(bf16[256,960]{0,1:T(8,128)(2,1)S(1)} %copy-done.3, bf16[256,2560]{1,0:T(8,128)(2,1)} %copy-done.11), kind=kOutput, calls=%fused_computation | convolution fusion | flops 1260748800 | bytes 6717440 | tf_op jit(solution)/shard_map/dot_general | solution.py:26
  185.6 7.9 %copy.24 = bf16[2560,960]{1,0:T(8,128)(2,1)} copy(bf16[2560,960]{0,1:T(8,128)(2,1)} %convolution_convert_fusion) | data formatting | bytes 9830400 | tf_op jit(solution)/shard_map/convert_element_type | solution.py:612
  193.4 3.6 convolution_convert_fusion.1
  197.0 8.0 %copy.23 = bf16[2560,960]{1,0:T(8,128)(2,1)} copy(bf16[2560,960]{0,1:T(8,128)(2,1)} %convolution_convert_fusion.1) | data formatting | bytes 9830400 | tf_op jit(solution)/shard_map/convert_element_type | solution.py:612
  205.0 3.6 convolution_convert_fusion.2
  208.7 7.9 %copy.22 = bf16[2560,960]{1,0:T(8,128)(2,1)} copy(bf16[2560,960]{0,1:T(8,128)(2,1)} %convolution_convert_fusion.2) | data formatting | bytes 9830400 | tf_op jit(solution)/shard_map/convert_element_type | solution.py:612
  216.5 184.9 %scatter_all.1 = (f32[80,960]{1,0:T(8,128)}, f32[80,960]{1,0:T(8,128)}, f32[80,960]{1,0:T(8,128)}, f32[80,960]{1,0:T(8,128)}, f32[8,128]{1,0:T(8,128)}) custom-call(bf16[4,2,2,2,80,960]{5,4,3,2,1,0:T(8,128)(2,1)} %bitcast.120, bf16[4,2,2,2,80,960]{5,4,3,2,1,0:T(8,128)(2,1)} %bitcast.123, bf16[4,2,2,2,80,960]{5,4,3,2,1,0:T(8,128)(2,1)} %bitcast.122, ...), custom_call_target="tpu_custom_call" | custom-call | tf_op jit(solution)/shard_map/scatter_all/pallas_call | solution.py:575
  401.4 1.2 slice_bitcast_fusion
  402.6 1.7 copy.38
  404.3 1.7 copy.39
  406.0 1.7 copy.40
  407.8 1.7 copy.41
  (60 shorter events, 0.3 us)
Async XLA Ops:
  126.8 1.9 copy-start.12
  127.0 1.1 copy-start.7
  128.1 2.0 copy-start
  128.1 6.3 %slice-start = ((s8[5242880]{0:T(1024)(128)(4,1)}), s8[4194304]{0:T(1024)(128)(4,1)S(1)}, s32[]{:S(2)}) async-start(s8[5242880]{0:T(1024)(128)(4,1)} %bitcast.127), calls=%async_computation | async-start | bytes 8388608
  128.8 2.9 copy-start.4
  128.8 5.6 %slice-start.1 = ((s8[5242880]{0:T(1024)(128)(4,1)}), s8[1048576]{0:T(1024)(128)(4,1)S(1)}, s32[]{:S(2)}) async-start(s8[5242880]{0:T(1024)(128)(4,1)} %bitcast.127), calls=%async_computation.1 | async-start | bytes 2097152
  130.1 4.0 copy-start.6
  134.2 2.2 slice-start.4
  134.4 2.3 slice-start.5
  134.5 5.5 %slice-start.6 = ((s8[5242880]{0:T(1024)(128)(4,1)}), s8[4194304]{0:T(1024)(128)(4,1)S(1)}, s32[]{:S(2)}) async-start(s8[5242880]{0:T(1024)(128)(4,1)} %bitcast.169), calls=%async_computation.6 | async-start | bytes 8388608
  136.7 3.2 copy-start.2
  136.7 3.2 slice-start.7
  144.4 3.0 copy-start.11
  144.4 3.0 copy-start.9
  152.3 3.6 copy-start.1
  152.3 4.4 %copy-start.13 = (bf16[256,320]{0,1:T(8,128)(2,1)S(1)}, bf16[256,320]{0,1:T(8,128)(2,1)}, u32[]{:S(2)}) copy-start(bf16[256,320]{0,1:T(8,128)(2,1)} %copy-done.12) | copy-start | bytes 491524
  156.7 2.9 copy-start.17
  156.8 1.9 copy-start.8
  156.8 2.9 slice-start.2
  158.6 2.2 slice-start.3
  159.1 2.0 copy-start.5
  159.2 3.6 copy-start.15
  161.1 1.7 copy-start.14
  162.8 4.0 copy-start.16
  172.6 7.9 %copy-start.3 = (bf16[256,960]{0,1:T(8,128)(2,1)S(1)}, bf16[256,960]{0,1:T(8,128)(2,1)}, u32[]{:S(2)}) copy-start(bf16[256,960]{0,1:T(8,128)(2,1)} %param.10) | copy-start | bytes 1474564
  197.0 8.0 %copy-start.10 = (bf16[256,2560]{1,0:T(8,128)(2,1)S(1)}, bf16[256,2560]{1,0:T(8,128)(2,1)}, u32[]{:S(2)}) copy-start(bf16[256,2560]{1,0:T(8,128)(2,1)} %copy-done.9) | copy-start | bytes 3932164
